TPU v7x, 32 devices: a whole 2x2x4 slice. The times are simulated.
32 devices in a mesh: dom: 2 (over y), row: 4 (over z), sub: 2 (over x), rep: 2 (over core).
Axes of the slice: x: 2, y: 2, z: 4, core: 2. Of those that a mesh axis runs over, the one named last changes fastest.
Arguments:
- vectors: bfloat16 [28672, 768], P(('dom', 'row', 'sub', 'rep')), parts along dimension 0, may hold values from -150 to 150
- rotation: bfloat16 [1536, 768], P('dom'), parts along dimension 0, may hold values from -0.21875 to 0.21875
- codebooks: float32 [96, 256, 16], P(('dom', 'sub')), parts along dimension 0, may hold values from -8 to 8
Outputs:
- reconstruction: bfloat16 [28672, 768], P(('dom', 'row', 'sub', 'rep')), parts along dimension 0
- new_codebooks: float32 [96, 256, 16], P(('dom', 'sub')), parts along dimension 0
- cross_cov: float32 [1536, 768], P(('dom', 'sub')), parts along dimension 0
There are 2 independent parts, one for each index of `dom`. A program takes and returns all parts, laid end to end along the dimension named above; each array names one. Nothing has to cross between parts.
All inputs are finite; a program needn't handle non-finite values.
Results may differ from a plain program's by a relative error of at most 0.012.
Values may be sent and summed in bfloat16 or wider, within the bound.
No kernel may reach another device: no remote copies, remote signals or barrier semaphores. Data moves between devices by JAX's collectives and lax.ppermute only.
A program may use at most 64 MiB of HBM per device.

v0:
```python
import jax
import jax.numpy as jnp
from jax import lax
from jax.sharding import PartitionSpec as P

SUBDIM = 16
softness_scale = 4.0


def quantize_rows(block, codebook):
    block = block.astype(jnp.float32)
    cross_product = jnp.dot(codebook, block, precision=lax.Precision.HIGHEST)
    squared_norms = jnp.sum(codebook * codebook, axis=1)
    affinity_scores = (2.0 * cross_product - squared_norms[:, None]) / softness_scale
    weights = jax.nn.softmax(affinity_scores, axis=0)
    recon = jnp.dot(codebook.T, weights, precision=lax.Precision.HIGHEST)
    sums = lax.dot_general(
        weights, block, (((1,), (1,)), ((), ())), precision=lax.Precision.HIGHEST
    )
    counts = jnp.sum(weights, axis=1)
    return (recon, sums, counts)


def on_device(vectors, rotation, codebooks):
    row_count = vectors.shape[0]
    width = vectors.shape[1]
    groups = lax.axis_size("sub")
    group_width = width // groups
    rotated_t = lax.dot_general(
        rotation, vectors, (((0,), (1,)), ((), ())), preferred_element_type=jnp.float32
    ).astype(jnp.bfloat16)
    grouped = rotated_t.reshape(groups, group_width, row_count)
    received = lax.all_to_all(grouped, "sub", split_axis=0, concat_axis=2, tiled=True)
    columns = received.shape[2]
    blocks = received.reshape(group_width // SUBDIM, SUBDIM, columns)
    recon, sums_local, counts_local = lax.map(
        lambda pair: quantize_rows(pair[0], pair[1]), (blocks, codebooks)
    )
    recon_sent = recon.astype(jnp.bfloat16).reshape(1, group_width, columns)
    returned = lax.all_to_all(recon_sent, "sub", split_axis=2, concat_axis=0, tiled=True)
    recon_t = returned.reshape(width, row_count)
    total = row_count * lax.axis_size("row") * groups * lax.axis_size("rep")
    code_sums, counts = lax.psum((sums_local, counts_local), ("row", "rep"))
    partial_term = lax.dot_general(
        vectors, recon_t, (((0,), (1,)), ((), ())), preferred_element_type=jnp.float32
    )
    whole_cross = lax.psum(partial_term, ("row", "sub", "rep"))
    cross_rows = lax.dynamic_slice_in_dim(
        whole_cross, lax.axis_index("sub") * group_width, group_width, 0
    )
    new_codebooks = (code_sums + codebooks) / (counts[:, :, None] + 1.0)
    reconstruction = recon_t.T
    return (reconstruction, new_codebooks, cross_rows / total)


def solution(mesh):
    placed = (P(("dom", "row", "sub", "rep"), None), P("dom", None), P(("dom", "sub"), None, None))
    return jax.shard_map(
        on_device,
        mesh=mesh,
        in_specs=placed,
        out_specs=(
            P(("dom", "row", "sub", "rep"), None),
            P(("dom", "sub"), None, None),
            P(("dom", "sub"), None),
        ),
        check_vma=False,
    )
```

profile of v0, /device:TPU:0, one launch (start us, length us, event | category | flops | bytes accessed | tf_op | source)
XLA Modules:
  0.0 368.6 jit_solution(16869227199885064852)
XLA Ops:
  8.5 3.8 %convolution_convert_fusion = bf16[768,896]{1,0:T(8,128)(2,1)} fusion(bf16[768,768]{1,0:T(8,128)(2,1)} %param.6, bf16[896,768]{1,0:T(8,128)(2,1)S(1)} %copy-done), kind=kOutput, calls=%fused_computation.25 | convolution fusion | flops 1057652736 | bytes 3932160 | tf_op jit(solution)/shard_map/dot_general | solution.py:29
  12.3 4.2 %all-to-all-start = ((bf16[2,384,896]{2,1,0:T(8,128)(2,1)}), bf16[2,384,896]{2,1,0:T(8,128)(2,1)S(1)}, u32[]{:S(2)}, u32[]{:S(2)}) async-start(bf16[2,384,896]{2,1,0:T(8,128)(2,1)} %bitcast.68), calls=%async_computation | async-start | bytes 2752512 | tf_op jit(solution)/shard_map/all_to_all | solution.py:33
  16.5 18.0 %all-to-all-done = bf16[2,384,896]{2,1,0:T(8,128)(2,1)S(1)} async-done(((bf16[2,384,896]{2,1,0:T(8,128)(2,1)}), bf16[2,384,896]{2,1,0:T(8,128)(2,1)S(1)}, u32[]{:S(2)}, u32[]{:S(2)}) %all-to-all-start) | async-done | bytes 1376288 | tf_op jit(solution)/shard_map/all_to_all | solution.py:33
  34.5 2.5 copy.16
  37.0 3.5 reshape.26
  40.5 130.4 %while.14 = (s32[]{:T(128)}, bf16[24,16,1792]{2,1,0:T(8,128)(2,1)}, f32[24,256,16]{1,2,0:T(8,128)}, f32[24,256]{1,0:T(8,128)S(1)}, f32[24,256,16]{1,2,0:T(8,128)...) while((s32[]{:T(128)}, bf16[24,16,1792]{2,1,0:T(8,128)(2,1)}, f32[24,256,16]{1,2,0:T(8,128)}, ...), condition=%wide.region_5.6_spmd, body=%wide.region_0.5_spmd.sunk | while | flops 270209024 | bytes 9546853 | solution.py:36
  41.9 1.8 fusion.43
  47.4 1.8 fusion.43
  63.7 1.8 fusion.43
  69.1 1.8 fusion.43
  80.0 1.8 fusion.43
  85.4 1.8 fusion.43
  96.3 1.8 fusion.43
  101.7 1.8 fusion.43
  118.0 1.8 fusion.43
  123.4 1.8 fusion.43
  134.3 1.8 fusion.43
  139.7 1.8 fusion.43
  145.2 1.8 fusion.43
  150.6 1.8 fusion.43
  156.0 1.8 fusion.43
  170.9 7.0 %copy.17 = bf16[1,384,1792]{1,0,2:T(2,128)(2,1)} copy(bf16[1,384,1792]{2,1,0:T(8,128)(2,1)} %bitcast.67) | data formatting | bytes 2752512 | tf_op jit(solution)/shard_map/reshape | solution.py:39
  178.4 12.4 %reduce = bf16[1792,384]{1,0:T(8,128)(2,1)S(1)} reduce(bf16[1792,1,384]{2,1,0:T(2,128)(2,1)} %bitcast.61, bf16[]{:T(256)} %broadcast.16), dimensions={1}, to_apply=%bitcast.35.reduce_sub_computation | reduce | bytes 2752514
  192.0 3.6 all-to-all-start.1
  196.7 15.8 %all-to-all-done.1 = bf16[2,2,172032]{2,1,0:T(2,128)(2,1)S(1)} async-done(((bf16[2,2,172032]{2,1,0:T(2,128)(2,1)}), bf16[2,2,172032]{2,1,0:T(2,128)(2,1)S(1)}, u32[]{:S(2)}, u32[]{:S(2)}) %all-to-all-start.1) | async-done | bytes 1376288 | tf_op jit(solution)/shard_map/all_to_all | solution.py:40
  212.5 2.3 reshape.30
  214.8 3.1 copy.21
  219.7 2.8 convolution_bitcast_fusion.2
  222.5 27.0 %psum.22 = f32[24,256]{1,0:T(8,128)S(1)} all-reduce(f32[24,256]{1,0:T(8,128)S(1)} %get-tuple-element.39), channel_id=1, replica_groups=mesh['dom'=2,'row'=4,'sub'=2,'rep'=2] {'row','rep'}, use_global_device_ids=true, to_apply=%region_7.8 | all-reduce | flops 6144 | bytes 49152 | tf_op jit(solution)/shard_map/psum | solution.py:43
  249.5 7.6 %all-reduce.3.cloned.1.call-done = f32[24,256,16]{1,2,0:T(8,128)} async-done(((f32[24,256,16]{1,2,0:T(8,128)}), f32[24,256,16]{1,2,0:T(8,128)}) %all-reduce.3.cloned.1.call-update) | async-done | bytes 393232 | tf_op jit(solution)/shard_map/psum | solution.py:43
  257.1 1.8 add_divide_fusion
  260.4 98.6 %all-reduce.5.cloned.1.call-done = f32[768,768]{0,1:T(8,128)} async-done(((f32[768,768]{0,1:T(8,128)}), f32[768,768]{0,1:T(8,128)}) %all-reduce.5.cloned.1.call-update) | async-done | bytes 2359312 | tf_op jit(solution)/shard_map/psum | solution.py:47
  (171 shorter events, 112.6 us)
Async XLA Ops:
  7.2 1.3 copy-start
  12.3 22.2 %all-to-all-start = ((bf16[2,384,896]{2,1,0:T(8,128)(2,1)}), bf16[2,384,896]{2,1,0:T(8,128)(2,1)S(1)}, u32[]{:S(2)}, u32[]{:S(2)}) async-start(bf16[2,384,896]{2,1,0:T(8,128)(2,1)} %bitcast.68), calls=%async_computation | async-start | bytes 2752512 | tf_op jit(solution)/shard_map/all_to_all | solution.py:33
  37.0 3.5 copy-start.1
  192.0 20.5 %all-to-all-start.1 = ((bf16[2,2,172032]{2,1,0:T(2,128)(2,1)}), bf16[2,2,172032]{2,1,0:T(2,128)(2,1)S(1)}, u32[]{:S(2)}, u32[]{:S(2)}) async-start(bf16[2,2,172032]{2,1,0:T(2,128)(2,1)} %reshape.29), calls=%async_computation.1 | async-start | bytes 2752512 | tf_op jit(solution)/shard_map/all_to_all | solution.py:40
  195.7 61.4 %all-reduce.3.cloned.1.call-start = ((), (), s32[]{:S(2)}) async-start(), calls=%async_computation.2 | async-start | bytes 786432 | tf_op jit(solution)/shard_map/psum | solution.py:43
  196.4 162.6 %all-reduce.5.cloned.1.call-start = ((), (), s32[]{:S(2)}) async-start(), calls=%async_computation.3 | async-start | bytes 4718592 | tf_op jit(solution)/shard_map/psum | solution.py:47
Sparse Core Ops, SparseCore 0:
  199.4 57.6 all-reduce.2
  261.1 97.9 all-reduce.4
where the time goes:
time: 369 us
  waiting for transfers between devices  141 us (38%)
  matrix products  119 us (32%)
  other arithmetic  31.9 us (9%)
  local copies, waits for them, and re-layouts  27.1 us (7%)
  blocking collectives  27 us (7%)
  between operations  14.1 us (4%)
  starting transfers between devices  8.1 us (2%)
    psum x1, waiting for transfers between devices, on_device(): whole_cross = lax.psum(partial_term, ('row', 'sub', 'rep'))  98.6 us
    dot_general x24, matrix products, quantize_rows(): recon = jnp.dot(codebook.T, weights, precision=lax.Precision.HIGHEST)  43.4 us
    dot_general x24, matrix products, quantize_rows(): lax.dot_general(weights, block, (((1,), (1,)), ((), ())), precision=lax.P...  43.1 us
    psum x1, blocking collectives, on_device(): code_sums, counts = lax.psum((sums_local, counts_local), ('row', 'rep'))  27 us
    dot_general x24, matrix products, quantize_rows(): cross_product = jnp.dot(codebook, block, precision=lax.Precision.HIGHEST)  25.8 us
    all_to_all x1, waiting for transfers between devices, on_device(): lax.all_to_all(grouped, 'sub', split_axis=0, concat_axis=2, tiled=True)  18 us
    all_to_all x1, waiting for transfers between devices, on_device(): lax.all_to_all(recon_sent, 'sub', split_axis=2, concat_axis=0, tiled=True)  15.8 us
    unnamed x1, other arithmetic  12.4 us
  transfers between devices with their start and end apart: 4, of which 4 were waited for; matrix products, arithmetic and copies ran while one was open for 4% of the time, Pallas kernels for 0%

commit v1 on v0

--- a/solution.py
+++ b/solution.py
@@ -5,6 +5,12 @@
 
 SUBDIM = 16
 softness_scale = 4.0
+
+
+def swap_blocks(value, axis, split, join):
+    pieces = jnp.split(value, lax.axis_size(axis), axis=split)
+    received = lax.all_to_all(jnp.stack(pieces), axis, 0, 0)
+    return jnp.concatenate(received, axis=join)
 
 
 def quantize_rows(block, codebook):
@@ -37,7 +43,7 @@
         lambda pair: quantize_rows(pair[0], pair[1]), (blocks, codebooks)
     )
     recon_sent = recon.astype(jnp.bfloat16).reshape(1, group_width, columns)
-    returned = lax.all_to_all(recon_sent, "sub", split_axis=2, concat_axis=0, tiled=True)
+    returned = swap_blocks(recon_sent, "sub", 2, 0)
     recon_t = returned.reshape(width, row_count)
     total = row_count * lax.axis_size("row") * groups * lax.axis_size("rep")
     code_sums, counts = lax.psum((sums_local, counts_local), ("row", "rep"))

time: 369 us -> 351 us (0.951)
  local copies, waits for them, and re-layouts: 27.1 us -> 12.6 us
  other arithmetic: 31.9 us -> 20.8 us
  waiting for transfers between devices: 141 us -> 148 us
    unnamed x1 -> x0, other arithmetic: 12.4 us -> none
    unnamed x10 -> x5, local copies, waits for them, and re-layouts: 11.4 us -> 2.73 us
    psum x1, waiting for transfers between devices: 7.6 us -> 14.8 us  [on_device(): code_sums, counts = lax.psum((sums_local, counts_local), ('row', 'rep'))]
    reshape x1 -> x0, local copies, waits for them, and re-layouts: 6.95 us -> none  [on_device(): recon_sent = recon.astype(jnp.bfloat16).reshape(1, group_width, columns)]
  transfers between devices with their start and end apart: 4 -> 4, of which waited for: 4 -> 4; matrix products, arithmetic and copies ran while one was open for 4% -> 2% of each run, Pallas kernels for 0% -> 0%
where the time goes in v1:
time: 351 us; the launch traced here: 350 us
  waiting for transfers between devices  148 us (42%)
  matrix products  119 us (34%)
  blocking collectives  27 us (8%)
  other arithmetic  20.8 us (6%)
  between operations  14.1 us (4%)
  local copies, waits for them, and re-layouts  12.6 us (4%)
  starting transfers between devices  7.92 us (2%)
    psum x1, waiting for transfers between devices, on_device(): whole_cross = lax.psum(partial_term, ('row', 'sub', 'rep'))  98.6 us
    dot_general x24, matrix products, quantize_rows(): recon = jnp.dot(codebook.T, weights, precision=lax.Precision.HIGHEST)  43.4 us
    dot_general x24, matrix products, quantize_rows(): lax.dot_general(weights, block, (((1,), (1,)), ((), ())), precision=lax.P...  43.1 us
    psum x1, blocking collectives, on_device(): code_sums, counts = lax.psum((sums_local, counts_local), ('row', 'rep'))  27 us
    dot_general x24, matrix products, quantize_rows(): cross_product = jnp.dot(codebook, block, precision=lax.Precision.HIGHEST)  25.8 us
    all_to_all x1, waiting for transfers between devices, on_device(): lax.all_to_all(grouped, 'sub', split_axis=0, concat_axis=2, tiled=True)  18 us
    all_to_all x1, waiting for transfers between devices, swap_blocks(): received = lax.all_to_all(jnp.stack(pieces), axis, 0, 0)  16 us
    psum x1, waiting for transfers between devices, on_device(): code_sums, counts = lax.psum((sums_local, counts_local), ('row', 'rep'))  14.8 us
  transfers between devices with their start and end apart: 4, of which 4 were waited for; matrix products, arithmetic and copies ran while one was open for 2% of the time, Pallas kernels for 0%

profile of v1, /device:TPU:0, one launch (start us, length us, event | category | flops | bytes accessed | tf_op | source)
XLA Modules:
  0.0 350.2 jit_solution(15157292639542862401)
XLA Ops:
  8.5 3.8 %convolution_convert_fusion = bf16[768,896]{1,0:T(8,128)(2,1)} fusion(bf16[768,768]{1,0:T(8,128)(2,1)} %param.6, bf16[896,768]{1,0:T(8,128)(2,1)S(1)} %copy-done), kind=kOutput, calls=%fused_computation.25 | convolution fusion | flops 1057652736 | bytes 3932160 | tf_op jit(solution)/shard_map/dot_general | solution.py:35
  12.3 4.2 %all-to-all-start = ((bf16[2,384,896]{2,1,0:T(8,128)(2,1)}), bf16[2,384,896]{2,1,0:T(8,128)(2,1)S(1)}, u32[]{:S(2)}, u32[]{:S(2)}) async-start(bf16[2,384,896]{2,1,0:T(8,128)(2,1)} %bitcast.64), calls=%async_computation | async-start | bytes 2752512 | tf_op jit(solution)/shard_map/all_to_all | solution.py:39
  16.5 18.0 %all-to-all-done = bf16[2,384,896]{2,1,0:T(8,128)(2,1)S(1)} async-done(((bf16[2,384,896]{2,1,0:T(8,128)(2,1)}), bf16[2,384,896]{2,1,0:T(8,128)(2,1)S(1)}, u32[]{:S(2)}, u32[]{:S(2)}) %all-to-all-start) | async-done | bytes 1376288 | tf_op jit(solution)/shard_map/all_to_all | solution.py:39
  34.5 2.5 copy.10
  37.0 3.5 %reshape.22 = bf16[24,16,1792]{2,1,0:T(8,128)(2,1)S(1)} reshape(bf16[1,384,2,896]{3,2,1,0:T(2,128)(2,1)} %copy.10) | data formatting | bytes 2752512 | tf_op jit(solution)/shard_map/reshape | solution.py:41
  40.5 130.4 %while.14 = (s32[]{:T(128)}, bf16[24,16,1792]{2,1,0:T(8,128)(2,1)}, f32[24,256,16]{1,2,0:T(8,128)}, f32[24,256]{1,0:T(8,128)S(1)}, f32[24,256,16]{1,2,0:T(8,128)...) while((s32[]{:T(128)}, bf16[24,16,1792]{2,1,0:T(8,128)(2,1)}, f32[24,256,16]{1,2,0:T(8,128)}, ...), condition=%wide.region_5.6_spmd, body=%wide.region_0.5_spmd.sunk | while | flops 270209024 | bytes 9546853 | solution.py:42
  41.9 1.8 fusion.43
  47.4 1.8 fusion.43
  52.8 1.8 fusion.43
  58.2 1.8 fusion.43
  63.7 1.8 fusion.43
  69.1 1.8 fusion.43
  80.0 1.8 fusion.43
  85.4 1.8 fusion.43
  90.8 1.8 fusion.43
  96.3 1.8 fusion.43
  101.7 1.8 fusion.43
  107.1 1.8 fusion.43
  112.5 1.8 fusion.43
  118.0 1.8 fusion.43
  123.4 1.8 fusion.43
  139.7 1.8 fusion.43
  145.1 1.8 fusion.43
  156.0 1.8 fusion.43
  161.4 1.8 fusion.43
  173.6 3.6 %all-to-all-start.1 = ((bf16[2,1,384,896]{3,2,1,0:T(8,128)(2,1)}), bf16[2,1,384,896]{3,2,1,0:T(8,128)(2,1)S(1)}, u32[]{:S(2)}, u32[]{:S(2)}) async-start(bf16[2,1,384,896]{3,2,1,0:T(8,128)(2,1)} %pad_maximum_fusion), calls=%async_computation.1 | async-start | bytes 2752512 | tf_op jit(solution)/shard_map/all_to_all | solution.py:12
  178.0 16.0 %all-to-all-done.1 = bf16[2,1,384,896]{3,2,1,0:T(8,128)(2,1)S(1)} async-done(((bf16[2,1,384,896]{3,2,1,0:T(8,128)(2,1)}), bf16[2,1,384,896]{3,2,1,0:T(8,128)(2,1)S(1)}, u32[]{:S(2)}, u32[]{:S(2)}) %all-to-all-start.1) | async-done | bytes 1376288 | tf_op jit(solution)/shard_map/all_to_all | solution.py:12
  194.0 2.8 convolution_bitcast_fusion.2
  196.8 27.0 %psum.22 = f32[24,256]{1,0:T(8,128)S(1)} all-reduce(f32[24,256]{1,0:T(8,128)S(1)} %get-tuple-element.39), channel_id=1, replica_groups=mesh['dom'=2,'row'=4,'sub'=2,'rep'=2] {'row','rep'}, use_global_device_ids=true, to_apply=%region_7.8 | all-reduce | flops 6144 | bytes 49152 | tf_op jit(solution)/shard_map/psum | solution.py:49
  223.9 14.8 %all-reduce.3.cloned.1.call-done = f32[24,256,16]{1,2,0:T(8,128)} async-done(((f32[24,256,16]{1,2,0:T(8,128)}), f32[24,256,16]{1,2,0:T(8,128)}) %all-reduce.3.cloned.1.call-update) | async-done | bytes 393232 | tf_op jit(solution)/shard_map/psum | solution.py:49
  238.7 1.8 add_divide_fusion
  242.1 98.6 %all-reduce.5.cloned.1.call-done = f32[768,768]{0,1:T(8,128)} async-done(((f32[768,768]{0,1:T(8,128)}), f32[768,768]{0,1:T(8,128)}) %all-reduce.5.cloned.1.call-update) | async-done | bytes 2359312 | tf_op jit(solution)/shard_map/psum | solution.py:53
  (166 shorter events, 104.3 us)
Async XLA Ops:
  7.2 1.3 copy-start
  12.3 22.2 %all-to-all-start = ((bf16[2,384,896]{2,1,0:T(8,128)(2,1)}), bf16[2,384,896]{2,1,0:T(8,128)(2,1)S(1)}, u32[]{:S(2)}, u32[]{:S(2)}) async-start(bf16[2,384,896]{2,1,0:T(8,128)(2,1)} %bitcast.64), calls=%async_computation | async-start | bytes 2752512 | tf_op jit(solution)/shard_map/all_to_all | solution.py:39
  37.0 3.5 %copy-start.1 = (f32[24,256,16]{1,2,0:T(8,128)S(1)}, f32[24,256,16]{1,2,0:T(8,128)}, u32[]{:S(2)}) copy-start(f32[24,256,16]{1,2,0:T(8,128)} %param.7) | copy-start | bytes 1179652
  173.6 20.5 %all-to-all-start.1 = ((bf16[2,1,384,896]{3,2,1,0:T(8,128)(2,1)}), bf16[2,1,384,896]{3,2,1,0:T(8,128)(2,1)S(1)}, u32[]{:S(2)}, u32[]{:S(2)}) async-start(bf16[2,1,384,896]{3,2,1,0:T(8,128)(2,1)} %pad_maximum_fusion), calls=%async_computation.1 | async-start | bytes 2752512 | tf_op jit(solution)/shard_map/all_to_all | solution.py:12
  177.2 61.5 %all-reduce.3.cloned.1.call-start = ((), (), s32[]{:S(2)}) async-start(), calls=%async_computation.2 | async-start | bytes 786432 | tf_op jit(solution)/shard_map/psum | solution.py:49
  178.0 162.7 %all-reduce.5.cloned.1.call-start = ((), (), s32[]{:S(2)}) async-start(), calls=%async_computation.3 | async-start | bytes 4718592 | tf_op jit(solution)/shard_map/psum | solution.py:53
Sparse Core Ops, SparseCore 0:
  181.0 57.7 all-reduce.2
  242.7 97.9 all-reduce.4

commit v2 on v0

--- a/solution.py
+++ b/solution.py
@@ -44,7 +44,9 @@
     partial_term = lax.dot_general(
         vectors, recon_t, (((0,), (1,)), ((), ())), preferred_element_type=jnp.float32
     )
-    whole_cross = lax.psum(partial_term, ("row", "sub", "rep"))
+    whole_cross = partial_term
+    for over in (("sub", "rep"), "row"):
+        whole_cross = lax.psum(whole_cross, over)
     cross_rows = lax.dynamic_slice_in_dim(
         whole_cross, lax.axis_index("sub") * group_width, group_width, 0
     )

time: 369 us -> 444 us (1.20)
  waiting for transfers between devices: 141 us -> 198 us
  blocking collectives: 27 us -> 49 us
    psum x1 -> x2, waiting for transfers between devices: 98.6 us -> 149 us  [on_device(): whole_cross = lax.psum(whole_cross, over)]
    psum x1, waiting for transfers between devices: 7.6 us -> 30 us  [on_device(): code_sums, counts = lax.psum((sums_local, counts_local), ('row', 'rep'))]
    all_to_all x0 -> x1, blocking collectives: none -> 20.5 us  [on_device(): lax.all_to_all(recon_sent, 'sub', split_axis=2, concat_axis=0, tiled=True)]
    all_to_all x1 -> x0, waiting for transfers between devices: 15.8 us -> none  [on_device(): lax.all_to_all(recon_sent, 'sub', split_axis=2, concat_axis=0, tiled=True)]
  transfers between devices with their start and end apart: 4 -> 4, of which waited for: 4 -> 4; matrix products, arithmetic and copies ran while one was open for 4% -> 1% of each run, Pallas kernels for 0% -> 0%
where the time goes in v2:
time: 444 us; the launch traced here: 443 us
  waiting for transfers between devices  198 us (45%)
  matrix products  119 us (27%)
  blocking collectives  49 us (11%)
  other arithmetic  31.9 us (7%)
  local copies, waits for them, and re-layouts  27.1 us (6%)
  between operations  13.8 us (3%)
    psum x2, waiting for transfers between devices, on_device(): whole_cross = lax.psum(whole_cross, over)  149 us
    dot_general x24, matrix products, quantize_rows(): recon = jnp.dot(codebook.T, weights, precision=lax.Precision.HIGHEST)  43.4 us
    dot_general x24, matrix products, quantize_rows(): lax.dot_general(weights, block, (((1,), (1,)), ((), ())), precision=lax.P...  43.1 us
    psum x1, waiting for transfers between devices, on_device(): code_sums, counts = lax.psum((sums_local, counts_local), ('row', 'rep'))  30 us
    psum x1, blocking collectives, on_device(): code_sums, counts = lax.psum((sums_local, counts_local), ('row', 'rep'))  28.5 us
    dot_general x24, matrix products, quantize_rows(): cross_product = jnp.dot(codebook, block, precision=lax.Precision.HIGHEST)  25.8 us
    all_to_all x1, blocking collectives, on_device(): lax.all_to_all(recon_sent, 'sub', split_axis=2, concat_axis=0, tiled=True)  20.5 us
    all_to_all x1, waiting for transfers between devices, on_device(): lax.all_to_all(grouped, 'sub', split_axis=0, concat_axis=2, tiled=True)  18 us
  transfers between devices with their start and end apart: 4, of which 4 were waited for; matrix products, arithmetic and copies ran while one was open for 1% of the time, Pallas kernels for 0%

profile of v2, /device:TPU:0, one launch (start us, length us, event | category | flops | bytes accessed | tf_op | source)
XLA Modules:
  0.0 443.5 jit_solution(2538147988265519467)
XLA Ops:
  8.5 3.8 convolution_convert_fusion
  12.3 4.2 all-to-all-start
  16.5 18.0 %all-to-all-done = bf16[2,384,896]{2,1,0:T(8,128)(2,1)S(1)} async-done(((bf16[2,384,896]{2,1,0:T(8,128)(2,1)}), bf16[2,384,896]{2,1,0:T(8,128)(2,1)S(1)}, u32[]{:S(2)}, u32[]{:S(2)}) %all-to-all-start) | async-done | bytes 1376288 | tf_op jit(solution)/shard_map/all_to_all | solution.py:33
  34.5 2.5 copy.16
  37.0 3.5 reshape.26
  40.5 130.4 %while.14 = (s32[]{:T(128)}, bf16[24,16,1792]{2,1,0:T(8,128)(2,1)}, f32[24,256,16]{1,2,0:T(8,128)}, f32[24,256]{1,0:T(8,128)S(1)}, f32[24,256,16]{1,2,0:T(8,128)...) while((s32[]{:T(128)}, bf16[24,16,1792]{2,1,0:T(8,128)(2,1)}, f32[24,256,16]{1,2,0:T(8,128)}, ...), condition=%wide.region_5.6_spmd, body=%wide.region_0.5_spmd.sunk | while | flops 270209024 | bytes 9546853 | solution.py:36
  41.9 1.8 fusion.43
  47.4 1.8 fusion.43
  63.7 1.8 fusion.43
  69.1 1.8 fusion.43
  80.0 1.8 fusion.43
  85.4 1.8 fusion.43
  96.3 1.8 fusion.43
  101.7 1.8 fusion.43
  118.0 1.8 fusion.43
  123.4 1.8 fusion.43
  134.3 1.8 fusion.43
  139.7 1.8 fusion.43
  145.2 1.8 fusion.43
  150.6 1.8 fusion.43
  156.0 1.8 fusion.43
  170.9 7.0 %copy.17 = bf16[1,384,1792]{1,0,2:T(2,128)(2,1)} copy(bf16[1,384,1792]{2,1,0:T(8,128)(2,1)} %bitcast.67) | data formatting | bytes 2752512 | tf_op jit(solution)/shard_map/reshape | solution.py:39
  178.4 12.4 %reduce = bf16[1792,384]{1,0:T(8,128)(2,1)S(1)} reduce(bf16[1792,1,384]{2,1,0:T(2,128)(2,1)} %bitcast.61, bf16[]{:T(256)} %broadcast.16), dimensions={1}, to_apply=%bitcast.35.reduce_sub_computation | reduce | bytes 2752514
  192.0 20.5 %all_to_all.30 = bf16[2,2,172032]{2,1,0:T(2,128)(2,1)S(1)} all-to-all(bf16[2,2,172032]{2,1,0:T(2,128)(2,1)} %reshape.29), channel_id=1, replica_groups=mesh['dom'=2,'row'=4,'sub'=2,'rep'=2] {'sub'}, dimensions={0} | all-to-all | bytes 2752512 | tf_op jit(solution)/shard_map/all_to_all | solution.py:40
  212.5 2.3 reshape.30
  214.8 3.1 copy.21
  219.6 2.8 convolution_bitcast_fusion.2
  223.2 55.3 %all-reduce.6.cloned.1.call-done = f32[768,768]{0,1:T(8,128)} async-done(((f32[768,768]{0,1:T(8,128)}), f32[768,768]{0,1:T(8,128)}) %all-reduce.6.cloned.1.call-update) | async-done | bytes 2359312 | tf_op jit(solution)/shard_map/psum | solution.py:49
  278.5 28.5 %psum.29 = f32[24,256]{1,0:T(8,128)S(1)} all-reduce(f32[24,256]{1,0:T(8,128)S(1)} %get-tuple-element.39), channel_id=1, replica_groups=mesh['dom'=2,'row'=4,'sub'=2,'rep'=2] {'row','rep'}, use_global_device_ids=true, to_apply=%region_7.8 | all-reduce | flops 6144 | bytes 49152 | tf_op jit(solution)/shard_map/psum | solution.py:43
  307.1 30.0 %all-reduce.4.cloned.1.call-done = f32[24,256,16]{1,2,0:T(8,128)} async-done(((f32[24,256,16]{1,2,0:T(8,128)}), f32[24,256,16]{1,2,0:T(8,128)}) %all-reduce.4.cloned.1.call-update) | async-done | bytes 393232 | tf_op jit(solution)/shard_map/psum | solution.py:43
  337.0 1.8 add_divide_fusion
  340.4 93.8 %all-reduce.8.cloned.1.call-done = f32[768,768]{0,1:T(8,128)} async-done(((f32[768,768]{0,1:T(8,128)}), f32[768,768]{0,1:T(8,128)}) %all-reduce.8.cloned.1.call-update) | async-done | bytes 2359312 | tf_op jit(solution)/shard_map/psum | solution.py:49
  (173 shorter events, 112.5 us)
Async XLA Ops:
  7.2 1.3 copy-start
  12.3 22.2 %all-to-all-start = ((bf16[2,384,896]{2,1,0:T(8,128)(2,1)}), bf16[2,384,896]{2,1,0:T(8,128)(2,1)S(1)}, u32[]{:S(2)}, u32[]{:S(2)}) async-start(bf16[2,384,896]{2,1,0:T(8,128)(2,1)} %bitcast.68), calls=%async_computation | async-start | bytes 2752512 | tf_op jit(solution)/shard_map/all_to_all | solution.py:33
  16.5 262.0 %all-reduce.6.cloned.1.call-start = ((), (), s32[]{:S(2)}) async-start(), calls=%async_computation.3 | async-start | bytes 4718592 | tf_op jit(solution)/shard_map/psum | solution.py:49
  37.0 3.5 copy-start.1
  222.4 114.6 %all-reduce.4.cloned.1.call-start = ((), (), s32[]{:S(2)}) async-start(), calls=%async_computation.2 | async-start | bytes 786432 | tf_op jit(solution)/shard_map/psum | solution.py:43
  223.2 211.0 %all-reduce.8.cloned.1.call-start = ((), (), s32[]{:S(2)}) async-start(), calls=%async_computation.4 | async-start | bytes 4718592 | tf_op jit(solution)/shard_map/psum | solution.py:49
Sparse Core Ops, SparseCore 0:
  222.6 55.8 all-reduce.5
  281.4 55.5 all-reduce.3
  339.5 94.5 all-reduce.7
